TPU v7x, 32 devices: a whole 2x2x4 slice. The times are simulated.
32 devices in a mesh: dp: 8 (over z, x), mp: 4 (over y, core).
Axes of the slice: x: 2, y: 2, z: 4, core: 2. Of those that a mesh axis runs over, the one named last changes fastest.
Arguments:
- images: bfloat16 [128, 52, 768], P('dp'), may hold values from -6 to 6
- ln1_gain: bfloat16 [768], replicated, may hold values from 0.5 to 1.5
- ln1_bias: bfloat16 [768], replicated, may hold values from -1 to 1
- w_qkv: bfloat16 [768, 3, 768], P(None, None, 'mp'), may hold values from -0.21875 to 0.21875
- qv_bias: bfloat16 [2, 768], P(None, 'mp'), may hold values from -1 to 1
- w_out: bfloat16 [768, 768], P('mp'), may hold values from -0.625 to 0.625
- out_bias: bfloat16 [768], replicated, may hold values from -1 to 1
- ln2_gain: bfloat16 [768], replicated, may hold values from 0.5 to 1.5
- ln2_bias: bfloat16 [768], replicated, may hold values from -1 to 1
- w_fc1: bfloat16 [768, 3072], P(None, 'mp'), may hold values from -0.21875 to 0.21875
- fc1_bias: bfloat16 [3072], P('mp'), may hold values from -1.5 to 1.5
- w_fc2: bfloat16 [3072, 768], P('mp'), may hold values from -0.15625 to 0.15625
- fc2_bias: bfloat16 [768], replicated, may hold values from -1 to 1
- post_gain: float32 [768], replicated, may hold values from 0.5 to 1.5
- post_bias: float32 [768], replicated, may hold values from -1 to 1
- w_proj: float32 [768, 512], replicated, may hold values from -0.21875 to 0.21875
- captions: float32 [384, 512], P('dp'), may hold values from 0.01 to 0.1
- logit_scale: float32 [1], replicated, may hold values from 3 to 3.7
- caption_counts: int32 [128], P('dp'), may hold values from 1 to 5, as said below
- positives: int32 [128, 5], P('dp'), may hold values from -1 to 383, as said below
Outputs:
- loss: float32 [1], replicated
- block_out: bfloat16 [128, 52, 768], P('dp')
- images_grad: float32 [128, 52, 768], P('dp')
- ln1_gain_grad: float32 [768], replicated
- ln1_bias_grad: float32 [768], replicated
- w_qkv_grad: float32 [768, 3, 768], P(None, None, 'mp')
- qv_bias_grad: float32 [2, 768], P(None, 'mp')
- w_out_grad: float32 [768, 768], P('mp')
- out_bias_grad: float32 [768], replicated
- ln2_gain_grad: float32 [768], replicated
- ln2_bias_grad: float32 [768], replicated
- w_fc1_grad: float32 [768, 3072], P(None, 'mp')
- fc1_bias_grad: float32 [3072], P('mp')
- w_fc2_grad: float32 [3072, 768], P('mp')
- fc2_bias_grad: float32 [768], replicated
- post_gain_grad: float32 [768], replicated
- post_bias_grad: float32 [768], replicated
- w_proj_grad: float32 [768, 512], replicated
- captions_grad: float32 [384, 512], P('dp')
- logit_scale_grad: float32 [1], replicated
Inputs may be any that keep to these rules, and one draw needn't show every extreme that they name: `caption_counts`: the counts of all images sum to 384. `positives`: row i names the distinct captions of image i in its first caption_counts[i] places and holds -1 in the rest; every caption belongs to exactly one image.
All inputs are finite; a program needn't handle non-finite values.
Results may differ from a plain program's by a relative error of at most 0.03.
Values may be sent and summed in bfloat16 or wider, within the bound.
A program may use at most 128 MiB of HBM per device.

v0:
```python
import functools

import jax
import jax.numpy as jnp
from jax import lax
from jax.experimental import pallas as pl
from jax.experimental.pallas import tpu as pltpu
from jax.sharding import PartitionSpec as P

HEAD_DIM = 64
HIGH = lax.Precision.HIGHEST
F32 = jnp.float32
BF16 = jnp.bfloat16
MESH = pl.DeviceIdType.MESH
LOW = -1e30

G1, B1, G2, B2, OUTB, FC2B, PG, PB, FC1B, QB, VB, SCALE = range(12)
(LOSS, DG1, DB1, DQB, DVB, DOUTB, DG2, DB2, DFC1B, DFC2B, DPG, DPB) = range(12)


def norm_rows(values, gain, shift):
    centre = values - jnp.mean(values, -1, keepdims=True)
    spread = lax.rsqrt(jnp.mean(centre * centre, -1, keepdims=True) + 1e-05)
    scaled = centre * spread
    return (scaled * gain + shift, scaled, spread)


def norm_back(upper, gain, scaled, spread):
    inner = upper * gain
    return spread * (
        inner
        - jnp.mean(inner, -1, keepdims=True)
        - scaled * jnp.mean(inner * scaled, -1, keepdims=True)
    )


def dot(a, b, ca=1, cb=0, precision=None):
    return lax.dot_general(
        a, b, (((ca,), (cb,)), ((), ())), precision=precision, preferred_element_type=F32
    )


def iota(shape, dim):
    return lax.broadcasted_iota(jnp.int32, shape, dim)


def loop(count, step):
    if count == 1:
        step(0)
    else:
        lax.fori_loop(0, count, lambda i, c: (step(i), c)[1], 0)


def rows_at(index, size):
    if isinstance(index, int):
        return pl.ds(index * size, size)
    return pl.ds(pl.multiple_of(index * size, size), size)


class Named(dict):
    __getattr__ = dict.__getitem__


SEMS = 119


class Plan:
    def __init__(self, mesh_sizes, images, w_qkv, w_fc1, w_proj, captions, positives):
        self.dps, self.mps = mesh_sizes
        self.group, self.seq, self.width = images.shape
        self.rows = self.group * self.seq
        self.local = w_qkv.shape[2]
        self.heads = self.local // HEAD_DIM
        self.hg = self.heads * self.group
        self.hidden = w_fc1.shape[1]
        self.emb = w_proj.shape[1]
        self.images = self.group * self.dps
        self.own = captions.shape[0]
        self.captions = self.own * self.dps
        self.places = positives.shape[1]
        self.block = min(128, self.images)
        self.blocks = self.images // self.block
        self.part = self.images // self.mps
        self.quarter = self.rows // self.mps

    def semaphores(self):
        return SEMS + self.dps // 2 + (0 if self.blocks == 1 else 4)

    def operands(self):
        r, d, loc, hid = self.rows, self.width, self.local, self.hidden
        return dict(
            x_in=((r, d), BF16),
            wt_in=((3 * loc, d), BF16),
            wo_in=((loc, d), BF16),
            w1_in=((d, hid), BF16),
            w2_in=((hid, d), BF16),
            wp_in=((d, self.emb), F32),
            cap_in=((self.own, self.emb), F32),
            pos_in=((self.places, self.group), jnp.int32),
            count_in=((self.group,), jnp.int32),
            **{name + "_in": (s, t) for name, (s, t) in self.vectors().items()},
        )

    def vectors(self):
        d = self.width
        low = {name: ((d,), BF16) for name in ("g1", "b1", "g2", "b2", "ob", "f2b")}
        return dict(
            **low,
            pg=((d,), F32),
            pb=((d,), F32),
            f1b=((self.hidden,), BF16),
            qvb=((2, self.local), BF16),
            ls=((1,), F32),
        )

    def results(self):
        n, d, loc, hid = self.images, self.width, self.local, self.hidden
        return dict(
            block_out=((self.rows, d), BF16),
            images_out=((self.rows, d), BF16),
            small_out=((16, d), F32),
            cap_out=((self.own, self.emb), F32),
            post_out=((n, d), BF16),
            demb_out=((n, self.emb), BF16),
            act_out=((n, hid), BF16),
            dy_out=((n, d), BF16),
            mlp_out=((n, d), BF16),
            dpre_out=((n, hid), BF16),
            ctx_out=((n, loc), BF16),
            dmid_out=((n, d), BF16),
            a_out=((self.dps * self.hg, d), BF16),
            b_out=((self.dps * self.hg, d), BF16),
            dctx_out=((n, loc), BF16),
            ac_out=((n, d), BF16),
            qa_out=((n, loc), BF16),
        )

    def scratch(self):
        r, d, loc, hid = self.rows, self.width, self.local, self.hidden
        n, m, hg, b = self.images, self.mps, self.hg, self.block
        return dict(
            x=((r, d), BF16),
            vec=((16, d), F32),
            pos=((self.places, self.group), jnp.int32),
            count=((self.group,), jnp.int32),
            **self.vectors(),
            wt=((3 * loc, d), BF16),
            w1=((d, hid), BF16),
            w2=((hid, d), BF16),
            wpb=((d, self.emb), BF16),
            cap=((self.own, self.emb), F32),
            wo=((m * loc, d), BF16),
            attn=((r, d), BF16),
            hat=((r, d), BF16),
            spread=((r, 1), F32),
            q=((r, loc), BF16),
            k=((r, loc), BF16),
            v=((r, loc), BF16),
            q0=((64 * self.group, 128), F32),
            q1=((64 * self.group, 128), F32),
            k0=((64 * self.group, 128), F32),
            k1=((64 * self.group, 128), F32),
            v0=((64 * self.group, 128), F32),
            v1=((64 * self.group, 128), F32),
            probs=((hg, r), F32),
            plow=((hg, r), BF16),
            ca=((m, r, 128), BF16),
            cb=((m, r // 2, 128), BF16),
            mid=((r, d), F32),
            midq=((2, r // m, d), F32),
            part=((r, d), BF16),
            half=((r // 2, d), BF16),
            chip=((2, r // m, d), BF16),
            got=((2, r // m, d), BF16),
            blk=((r, d), BF16),
            xc=((n, d), BF16),
            plan=((n, 128), F32),
            text=((self.captions, self.emb), BF16),
            own=((self.own, self.emb), BF16),
            cg=((m, n, loc), BF16),
            midc=((n, d), F32),
            mlp=((b, d), BF16),
            pre=((n, hid), F32),
            act=((b, hid), BF16),
            part1=((n, d), BF16),
            sums=((4, n // 2, d), BF16),
            all1=((n, d), BF16),
            all2=((n, d), BF16),
            post=((b, d), BF16),
            unit=((n, self.emb), F32),
            stat=((n, 2), F32),
            low=((n, self.emb), BF16),
            lg=((b, self.captions), F32),
            dtext=((self.own, self.emb), F32),
            arow=((hg, d), BF16),
            brow=((hg, d), BF16),
            crow=((8, self.captions), F32),
            demb=((b, self.emb), BF16),
            dy=((b, d), BF16),
            dpre=((b, hid), BF16),
            dmid=((n, d), F32),
            dmidl=((b, d), BF16),
            dctx=((n, loc), BF16),
            capg=((self.own, self.emb), F32),
            small=((16, d), F32),
            ac=((b, d), BF16),
            qa=((b, loc), BF16),
            u=((m * 2 * hg, d), BF16),
            uq=((m * self.group, d), BF16),
            coef=((m * 2 * hg, 128), BF16),
            tot=((self.dps * 16, 128), BF16),
            sums_left=((16, 128), F32),
        )


def kernel(plan, *refs):
    names = [*plan.operands(), *plan.results(), *plan.scratch()]
    sems = refs[len(names)]
    used = iter(range(plan.semaphores()))

    places, free, ends = {}, [], []

    def sem():
        return sems.at[next(used)]

    def own():
        place = free.pop() if free else next(used)
        ref = sems.at[place]
        places[id(ref)] = (place, ref)
        return ref

    def done(copy):
        if copy.is_remote:
            copy.wait_send()
        else:
            copy.wait()
        free.append(places[id(copy.src_sem if copy.is_remote else copy.dst_sem)][0])

    def settle(count):
        for copy in ends[:count]:
            done(copy)
        del ends[:count]

    R = Named(zip(names, refs))
    rows, width, local, heads = plan.rows, plan.width, plan.local, plan.heads
    group, hg, dps, mps = plan.group, plan.hg, plan.dps, plan.mps
    dp, mp = lax.axis_index("dp"), lax.axis_index("mp")
    low_bit, high_bit = lax.rem(mp, 2), lax.div(mp, 2)
    near = mp + 1 - 2 * low_bit
    far = lax.rem(mp + 2, 4)
    put_sem = {n: own() for n in ("mlp", "act", "post", "demb", "dy", "dpre", "dmidl", "ac", "qa")}

    def dp_peer(i):
        return lax.rem(dp + dps + (i + 2) // 2 * (1 - 2 * (i % 2)), dps)

    def load(src, dst):
        copy = pltpu.make_async_copy(src, dst, own())
        copy.start()
        return copy

    def store(name, dst=None):
        ends.append(load(R[name], R[dst or name + "_out"]))

    def put(name, i, value):
        R[name][...] = value
        copy = pltpu.make_async_copy(
            R[name], R[name.removesuffix("l") + "_out"].at[rows_at(i, plan.block)], put_sem[name]
        )
        copy.start()
        if plan.blocks == 1:
            ends.append(copy)
        else:
            copy.wait()

    def send(src, dst, dp_to, mp_to, out, into):
        return pltpu.make_async_remote_copy(
            src_ref=src,
            dst_ref=dst,
            send_sem=out,
            recv_sem=into,
            device_id=(dp_to, mp_to),
            device_id_type=MESH,
        )

    class GatherDp:
        def __init__(self, buf, size, source=None):
            self.buf, self.size, self.source = buf, size, source
            self.out, self.into = own(), sem()

        def start(self):
            mine = self.buf.at[rows_at(dp, self.size)]
            source = mine if self.source is None else self.source

            def one(i):
                send(source, mine, dp_peer(i), mp, self.out, self.into).start()

            loop(dps - 1, one)
            rest = self.buf.at[pl.ds(0, (dps - 1) * self.size)]
            self.all = send(rest, rest, dp, near, self.out, self.into)
            ends.append(self.all)

        def wait(self):
            self.all.wait_recv()

    class GatherDpHalf:
        def __init__(self, buf, size, source):
            self.size, self.source = size, source
            self.out, self.into = own(), sem()
            half = buf.shape[1] // 2
            self.cols = pl.ds(pl.multiple_of(low_bit * half, 128), half)
            self.buf = buf.at[:, self.cols]
            self.near = send(self.buf, self.buf, dp, near, own(), sem())

        def start(self):
            source = self.source.at[:, self.cols]
            mine = self.buf.at[rows_at(dp, self.size)]
            self.own = load(source, mine)

            def one(i):
                send(source, mine, dp_peer(i), mp, self.out, self.into).start()

            loop(dps - 1, one)
            rest = self.buf.at[pl.ds(0, (dps - 1) * self.size)]
            self.all = send(rest, rest, dp, near, self.out, self.into)
            ends.append(self.all)

        def relay(self):
            done(self.own)
            self.all.wait_recv()
            self.near.start()
            ends.append(self.near)

        def wait(self):
            self.near.wait_recv()

    class GatherDpTwice:
        def __init__(self, buf, size, source):
            self.buf, self.size, self.source = buf, size, source
            self.out, self.into = own(), sem()
            self.beside = dp + 1 - 2 * lax.rem(dp, 2)
            self.arrive = [sem() for _ in range(dps // 2 - 1)]
            self.left = list(range(dps // 2 - 1))

        def at(self, i):
            return self.buf.at[rows_at(i, self.size)]

        def start(self):
            send(self.source, self.at(dp), self.beside, mp, self.out, self.into).start()
            for i, into in enumerate(self.arrive):
                send(self.source, self.at(dp), self.pair(i), mp, self.out, into).start()

        def pair(self, i):
            other, bit = lax.rem(dp, 2), 1
            while bit < dps // 2:
                other += 2 * bit * lax.rem(lax.div(dp, 2 * bit) + (i + 1) // bit, 2)
                bit *= 2
            return other

        def forward(self, part):
            count = len(self.arrive)
            for i in range(count * (part - 1) // 3, count * part // 3):
                block = self.at(self.pair(i))
                send(block, block, self.beside, mp, self.out, self.arrive[i]).wait_recv()
                send(block, block, self.beside, mp, self.out, self.into).start()

        def wait(self):
            half = self.buf.at[pl.ds(0, dps // 2 * self.size)]
            rest = self.buf.at[pl.ds(0, (dps - 1) * self.size)]
            send(half, half, self.beside, mp, self.out, self.into).wait_recv()
            ends.append(send(rest, rest, self.beside, mp, self.out, self.into))

    class GatherMp:
        def __init__(self, slot):
            self.slot = slot
            self.to_near = send(slot(mp), slot(mp), dp, near, own(), sem())
            self.to_far = send(slot(mp), slot(mp), dp, far, own(), sem())
            self.pass_on = send(slot(far), slot(far), dp, near, own(), sem())

        def start(self):
            self.to_far.start()
            self.to_near.start()
            ends.extend([self.to_near, self.to_far])

        def forward(self):
            self.to_far.wait_recv()
            self.pass_on.start()
            ends.append(self.pass_on)

        def wait(self):
            self.to_near.wait_recv()
            self.pass_on.wait_recv()

    class SumMp:
        def __init__(self, part, slots, got, total):
            self.part, self.slots, self.got, self.total = part, slots, got, total
            count = part.shape[0] // 2
            self.mine, other = rows_at(low_bit, count), rows_at(1 - low_bit, count)
            half = self.total.at[self.mine]
            self.first = send(part.at[other], slots.at[0], dp, near, own(), sem())
            self.second = send(slots.at[1], slots.at[got], dp, far, own(), sem())
            self.third = send(half, half, dp, near, own(), sem())

        def start(self):
            self.first.start()

        def middle(self):
            self.first.wait_recv()
            mine = self.part[self.mine, :].astype(F32)
            self.slots[1] = (mine + self.slots[0].astype(F32)).astype(BF16)
            self.second.start()

        def turn(self):
            self.second.wait_recv()
            done(self.second)
            total = self.slots[1].astype(F32) + self.slots[self.got].astype(F32)
            self.total[self.mine, :] = total.astype(BF16)
            self.third.start()
            ends.append(self.third)

        def wait(self):
            self.third.wait_recv()

    barrier = pltpu.get_barrier_semaphore()

    def greet(i):
        pl.semaphore_signal(
            barrier, inc=1, device_id=(lax.rem(dp + 1 + i, dps), mp), device_id_type=MESH
        )

    loop(dps - 1, greet)
    for i in range(1, mps):
        pl.semaphore_signal(
            barrier, inc=1, device_id=(dp, lax.rem(mp + i, mps)), device_id_type=MESH
        )
    vec = R.vec
    vectors = ("g1", "b1", "g2", "b2", "ob", "f2b", "pg", "pb", "f1b")
    got_first = [load(R[n + "_in"], R[n]) for n in ("x", "g1", "b1")]
    got_wo = load(R.wo_in, R.wo.at[rows_at(mp, local)])
    got_wt = load(R.wt_in, R.wt)
    got_small = [
        load(R[n + "_in"], R[n]) for n in (*vectors[2:], "qvb", "ls", "pos", "count", "cap")
    ]
    got_w1 = load(R.w1_in, R.w1)
    got_w2 = load(R.w2_in, R.w2)
    wp = R.mid.at[pl.ds(0, width), pl.ds(0, plan.emb)]
    got_wp = load(R.wp_in, wp)
    for name in ("small", "crow", "dtext", "q1"):
        R[name][...] = jnp.zeros_like(R[name])
    for name in ("v0", "v1"):
        R[name][rows : 64 * group, :] = jnp.zeros((64 * group - rows, 128), F32)

    def place(i):
        name = vectors[i]
        vec[i : i + 1, 0 : R[name].shape[0]] = R[name][...].astype(F32).reshape(1, -1)

    for got in got_first:
        done(got)
    place(0)
    place(1)

    def row(i, size=width):
        return vec[i : i + 1, 0:size]

    step = rows // 4

    def first_norm(i):
        at = rows_at(i, rows // 2)
        normed, hat, spread = norm_rows(R.x[at, :].astype(F32), row(G1), row(B1))
        R.spread[at, :] = spread
        R.attn[at, :] = normed.astype(BF16)
        R.hat[at, :] = hat.astype(BF16)

    loop(2, first_norm)
    for got in got_small:
        done(got)
    for i in range(2, len(vectors)):
        place(i)
    vec[QB : VB + 1, 0:local] = R.qvb[...].astype(F32)
    vec[SCALE : SCALE + 1, 0:1] = R.ls[...].reshape(1, 1)
    pl.semaphore_wait(barrier, dps - 1 + mps - 1)
    done(got_wo)
    gather_wo = GatherMp(lambda i: R.wo.at[rows_at(i, local)])
    gather_wo.start()
    done(got_wt)

    def project(i):
        at = rows_at(i, rows // 2)
        a = R.attn[at, :]
        for j, (name, shift) in enumerate((("q", QB), ("k", None), ("v", VB))):
            t = dot(a, R.wt[j * local : (j + 1) * local, :], 1, 1)
            if shift is not None:
                t = t + row(shift, local)
            t = t.astype(BF16)
            R[name][at, :] = t
            t = t.astype(F32)
            R[name + "0"][at, :] = t[:, 0:128]
            R[name + "1"][at, 0 : local - 128] = t[:, 128:local]

    loop(2, project)

    lane_head = iota((hg, local), 1) // HEAD_DIM
    own_head = lane_head == iota((hg, local), 0) // group

    def spread_heads(t):
        wide = jnp.concatenate([t.astype(F32)] * heads, 0)
        return jnp.where(own_head, wide, 0.0).astype(BF16)

    def join_heads(t):
        t = jnp.where(own_head, t, 0.0)
        total = t[0:group]
        for h in range(1, heads):
            total = total + t[h * group : (h + 1) * group]
        return total

    same = lax.rem(iota((hg, rows), 0), group) == lax.rem(iota((hg, rows), 1), group)
    qx = spread_heads(R.q[0:group, :])
    scores = jnp.where(same, dot(qx, R.k[...], 1, 1) * 0.125, LOW)
    weights = jnp.exp(scores - jnp.max(scores, -1, keepdims=True))
    probs = weights * (1.0 / jnp.sum(weights, -1, keepdims=True))
    R.probs[...] = probs
    R.plow[...] = probs.astype(BF16)
    mine = rows_at(dp, group)
    ctx = join_heads(dot(R.plow[...], R.v[...])).astype(BF16)
    cg = R.cg.at[mp]
    cg[mine, :] = ctx
    gather_ctx = GatherDp(cg, group)
    gather_ctx.start()
    gather_xc = GatherDpHalf(R.xc, group, R.x.at[pl.ds(0, group)])
    gather_xc.start()
    head_of = iota((128, 256), 1) // HEAD_DIM
    seen = iota((128, 128), 0) // 64 == iota((128, 128), 1) // 64
    seen &= lax.rem(iota((128, 128), 1), 64) < plan.seq

    def pair(t):
        both = [pl.ds(2 * t + j, 64, stride=group) for j in range(2)]

        def taken(name):
            parts = [R[name + i] for i in "01"]
            return jnp.concatenate(
                [jnp.concatenate([ref[at, :] for at in both], 0) for ref in parts], 1
            )

        qb = (taken("q") * 0.125).astype(BF16)
        kb, vb = taken("k"), taken("v")
        of_head = [head_of == h for h in range(heads)]
        k_wide = jnp.concatenate([jnp.where(m, kb, 0.0) for m in of_head], 0).astype(BF16)
        v_wide = jnp.concatenate([jnp.where(m, vb, 0.0) for m in of_head], 0).astype(BF16)
        scores = dot(qb, k_wide, 1, 1)
        scale = jnp.zeros((128, 256), F32)
        parts = []
        for h in range(heads):
            s = jnp.where(seen, scores[:, h * 128 : (h + 1) * 128], LOW)
            e = jnp.exp(s - jnp.max(s, -1, keepdims=True))
            scale = jnp.where(of_head[h], 1.0 / jnp.sum(e, -1, keepdims=True), scale)
            parts.append(e.astype(BF16))
        total = dot(jnp.concatenate(parts, 1), v_wide) * scale
        for j, at in enumerate(both):
            R.q0[at, :] = total[j * 64 : j * 64 + 64, 0:128]
            R.q1[at, :] = total[j * 64 : j * 64 + 64, 128:256]

    def attend(t):
        pair(2 * t)
        pair(2 * t + 1)

    first_part = 3 * group // 16
    loop(first_part, attend)
    table = [R.pos[...].astype(F32), R.count[...].astype(F32).reshape(1, group)]
    table = jnp.concatenate(table, 0)
    table = jnp.pad(table, ((0, 128 - table.shape[0]), (0, 128 - group)))
    R.plan[rows_at(dp, group), :] = table.T[0:group]
    gather_plan = GatherDp(R.plan, group)
    gather_plan.start()
    cap = R.cap[...]
    cap_factor = lax.rsqrt(jnp.sum(cap * cap, -1, keepdims=True) + 1e-06)
    R.own[...] = (cap * cap_factor).astype(BF16)
    gather_text = GatherDpHalf(R.text, plan.own, R.own)
    gather_text.start()
    gather_ctx.wait()
    gather_cg = GatherMp(lambda i: R.cg.at[i])
    gather_cg.start()
    loop(group // 4 - first_part, lambda t: attend(t + first_part))
    quarter = plan.quarter
    for i, index in enumerate((0, 2, 1, 3)):
        taken_rows = R.q0[index * quarter : (index + 1) * quarter, :]
        R.ca[mp, i * quarter : (i + 1) * quarter, :] = taken_rows.astype(BF16)
    R.cb[mp] = jnp.concatenate(
        [R.q1[0 : rows // 2, 0:64], R.q1[rows // 2 : rows, 0:64]], 1
    ).astype(BF16)

    class GatherSet:
        def __init__(self, i):
            wide, packed = pl.ds(2 * i * quarter, 2 * quarter), pl.ds(i * quarter, quarter)
            self.parts = (
                GatherMp(lambda m: R.ca.at[m, wide]),
                GatherMp(lambda m: R.cb.at[m, packed]),
            )

        def start(self):
            for part in self.parts:
                part.start()

        def forward(self):
            for part in self.parts:
                part.forward()

        def wait(self):
            for part in self.parts:
                part.wait()

    gather_sets = [GatherSet(i) for i in range(2)]
    gather_uk = GatherMp(lambda i: R.u.at[rows_at(i, hg)])
    gather_pc = GatherMp(lambda i: R.coef.at[rows_at(mps + i, hg)])
    gather_xc.relay()
    R.brow[...] = dot(R.plow[...], R.attn[...]).astype(BF16)
    uk = dot(qx, R.wt[local : 2 * local, :])
    R.u[rows_at(mp, hg), :] = uk.astype(BF16)
    fold = jnp.where(
        iota((rows, 128), 0) // group == iota((rows, 128), 1), 1.0, 0.0
    ).astype(BF16)
    late = rows_at(mps + mp, hg)
    R.coef[late, :] = dot(R.plow[...], fold).astype(BF16)
    gather_wo.forward()
    gather_cg.forward()
    for g in (gather_sets[0], gather_uk, gather_pc):
        g.start()
    gather_wo.wait()
    done(got_w1)
    done(got_w2)
    gather_xc.wait()
    gather_cg.wait()

    def class_forward(i):
        at = rows_at(i, plan.block)
        total = R.xc[at, :].astype(F32) + row(OUTB)
        joined = jnp.concatenate([R.cg[m, at, :].astype(F32) for m in range(mps)], 1)
        total += dot(joined.astype(BF16), R.wo[...])
        R.midc[at, :] = total
        mlp = norm_rows(total, row(G2), row(B2))[0].astype(BF16)
        put("mlp", i, mlp)
        pre = dot(mlp, R.w1[...]) + row(FC1B, plan.hidden)
        R.pre[at, :] = pre
        act = (pre * jax.nn.sigmoid(1.702 * pre)).astype(BF16)
        put("act", i, act)
        R.part1[at, :] = dot(act, R.w2[...]).astype(BF16)

    loop(plan.blocks, class_forward)
    sum1 = SumMp(R.part1, R.sums, 2, R.all1)
    sum1.start()

    size = plan.quarter

    def joined_context(index):
        side, which = lax.div(index, 2), lax.rem(index, 2)
        joined = []
        for m in range(mps):
            tail = R.cb[m, rows_at(which, size), :].astype(F32)
            tail = jnp.where(side == 0, tail[:, 0:64], tail[:, 64:128])
            joined += [R.ca[m, rows_at(2 * which + side, size), :].astype(F32), tail]
        return jnp.concatenate(joined, 1).astype(BF16)

    def bulk(i):
        at = [rows_at(index, size) for index in (others[i], owned[i])]
        total = jnp.concatenate([R.x[a, :].astype(F32) for a in at], 0) + row(OUTB)
        joined = [joined_context(index) for index in (others[i], owned[i])]
        total += dot(jnp.concatenate(joined, 0), R.wo[...])
        R.midq[i] = total[size : 2 * size]
        mlp = norm_rows(total, row(G2), row(B2))[0].astype(BF16)
        pre = dot(mlp, R.w1[...]) + row(FC1B, plan.hidden)
        act = (pre * jax.nn.sigmoid(1.702 * pre)).astype(BF16)
        part = dot(act, R.w2[...]).astype(BF16)
        R.part[at[0], :] = part[0:size]
        R.part[at[1], :] = part[size : 2 * size]

    others = [2 * (1 - low_bit) + i for i in range(2)]
    owned = [2 * low_bit + i for i in range(2)]
    def cut_rows(*counts):
        starts = [sum(counts[:n]) for n in range(len(counts))]
        return [pl.ds(a, c) for a, c in zip(starts, counts)]

    pieces = [cut_rows(96, size - 96), cut_rows(64, 96, size - 160)]

    def near_move(i):
        rows_other = R.part.at[rows_at(others[i], size)]
        return send(rows_other, R.half.at[pl.ds(i * size, size)], dp, near, own(), sem())

    def far_move(i, p):
        return send(R.chip.at[i, p], R.got.at[i, p], dp, far, own(), sem())

    to_near = [near_move(i) for i in range(2)]
    to_far = [[far_move(i, p) for p in pieces[i]] for i in range(2)]

    def chip_sum(i):
        to_near[i].wait_recv()
        mine = R.part[rows_at(owned[i], size), :].astype(F32)
        R.chip[i] = (mine + R.half[i * size : (i + 1) * size, :].astype(F32)).astype(BF16)

    def block_rows(index, p):
        return pl.ds(pl.multiple_of(index * size + p.start, 16), p.size)

    def near_block(i, p):
        at = R.blk.at[block_rows(owned[i], p)]
        return send(at, at, dp, near, own(), sem())

    blk_near = [[near_block(i, p) for p in pieces[i]] for i in range(2)]

    def store_rows(index, p):
        at = block_rows(index, p)
        ends.append(load(R.blk.at[at], R.block_out.at[at]))

    def finish(i):
        for n, p in enumerate(pieces[i]):
            to_far[i][n].wait_recv()
            total = R.chip[i, p, :].astype(F32) + R.got[i, p, :].astype(F32)
            total += R.midq[i, p, :] + row(FC2B)
            R.blk[block_rows(owned[i], p), :] = total.astype(BF16)
            blk_near[i][n].start()
            store_rows(owned[i], p)

    def class_queries(i):
        normed = norm_rows(R.xc[rows_at(i, plan.block), :].astype(F32), row(G1), row(B1))[0]
        normed = normed.astype(BF16)
        put("ac", i, normed)
        queries = dot(normed, R.wt[0:local, :], 1, 1) + row(QB, local)
        put("qa", i, queries.astype(BF16))

    loop(plan.blocks, class_queries)
    sum1.middle()
    done(got_wp)
    R.wpb[...] = wp[...].astype(BF16)
    gather_sets[0].forward()
    gather_text.relay()
    gather_sets[0].wait()
    started = len(ends)
    gather_sets[1].start()
    gather_b = GatherDp(R.b_out, hg, R.brow)
    gather_b.start()
    ends.append(load(R.brow, R.b_out.at[rows_at(dp, hg)]))
    bulk(0)
    sum1.turn()
    to_near[0].start()
    gather_plan.wait()
    gather_text.wait()
    sum1.wait()
    settle(started)

    done(sum1.first)
    scale = jnp.exp(row(SCALE, 1))
    crow = R.crow
    crow[0:1, :] = jnp.full((1, plan.captions), LOW, F32)

    def class_out(at):
        return R.midc[at, :] + R.all1[at, :].astype(F32) + row(FC2B)

    def logits_at(at):
        if plan.blocks == 1:
            return R.lg[...]
        return scale * dot(R.low[at, :], R.text[...], 1, 1)

    def head(i):
        at = rows_at(i, plan.block)
        post = norm_rows(class_out(at), row(PG), row(PB))[0]
        put("post", i, post.astype(BF16))
        emb = dot(post.astype(BF16), R.wpb[...])
        factor = lax.rsqrt(jnp.sum(emb * emb, -1, keepdims=True) + 1e-06)
        R.stat[at, 0:1] = factor
        unit = emb * factor
        R.unit[at, :] = unit
        image_low = unit.astype(BF16)
        R.low[at, :] = image_low
        logits = scale * dot(image_low, R.text[...], 1, 1)
        R.lg[...] = logits
        crow[0:1, :] = jnp.maximum(crow[0:1, :], jnp.max(logits, 0, keepdims=True))

    loop(plan.blocks, head)
    chip_sum(0)
    to_far[0][0].start()

    def matches(at):
        ids = iota((plan.block, plan.captions), 1).astype(F32)
        found = R.plan[at, 0:1] == ids
        for place in range(1, plan.places):
            found |= R.plan[at, place : place + 1] == ids
        return jnp.where(found, 1.0, 0.0)

    def put_small(i, value):
        R.small[i : i + 1, 0 : value.shape[1]] += value

    half_i, half_c = 0.5 / plan.images, 0.5 / plan.captions

    def stats(i):
        at = rows_at(i, plan.block)
        logits = logits_at(at)
        matched = matches(at) * logits
        crow[1:2, :] += jnp.sum(jnp.exp(logits - crow[0:1, :]), 0, keepdims=True)
        crow[2:3, :] += jnp.sum(matched, 0, keepdims=True)
        top = jnp.max(logits, 1, keepdims=True)
        lse = top + jnp.log(jnp.sum(jnp.exp(logits - top), 1, keepdims=True))
        R.stat[at, 1:2] = lse
        counts = R.plan[at, plan.places : plan.places + 1]
        terms = lse - jnp.sum(matched, 1, keepdims=True) / counts
        put_small(LOSS, half_i * jnp.sum(terms, 0, keepdims=True))

    loop(plan.blocks, stats)
    crow[3:4, :] = crow[0:1, :] + jnp.log(crow[1:2, :])
    put_small(LOSS, half_c * jnp.sum(crow[3:4, :] - crow[2:3, :], 1, keepdims=True))

    shape = (plan.captions, plan.own)
    own_captions = iota(shape, 0) == iota(shape, 1) + dp * plan.own
    own_captions = jnp.where(own_captions, 1.0, 0.0).astype(BF16)

    def head_back(i):
        at = rows_at(i, plan.block)
        logits = logits_at(at)
        match = matches(at)
        counts = R.plan[at, plan.places : plan.places + 1]
        dlog = half_i * (jnp.exp(logits - R.stat[at, 1:2]) - match / counts)
        dlog += half_c * (jnp.exp(logits - crow[3:4, :]) - match)
        dlow = dlog.astype(BF16)
        both = jnp.sum(dlow.astype(F32) * logits, 1, keepdims=True)
        R.small[LOSS : LOSS + 1, 128:129] += jnp.sum(both, 0, keepdims=True)
        dimage = scale * dot(dlow, R.text[...])
        own = dot(dlow, own_captions).astype(BF16)
        R.dtext[...] += dot(own, R.low[at, :], 0, 0)
        unit = R.unit[at, :]
        demb = R.stat[at, 0:1] * (dimage - unit * jnp.sum(unit * dimage, -1, keepdims=True))
        put("demb", i, demb.astype(BF16))
        dpost = dot(demb.astype(BF16), R.wpb[...], 1, 1)
        _, hat, spread = norm_rows(class_out(at), row(PG), row(PB))
        dcls = norm_back(dpost, row(PG), hat, spread)
        put_small(DPG, jnp.sum(dpost * hat, 0, keepdims=True))
        put_small(DPB, jnp.sum(dpost, 0, keepdims=True))
        put_small(DFC2B, jnp.sum(dcls, 0, keepdims=True))
        R.dmid[at, :] = dcls
        dy = dcls.astype(BF16)
        put("dy", i, dy)
        pre = R.pre[at, :]
        sigma = jax.nn.sigmoid(1.702 * pre)
        slope = sigma + 1.702 * pre * sigma * (1.0 - sigma)
        dpre = (dot(dy, R.w2[...], 1, 1) * slope).astype(BF16)
        put("dpre", i, dpre)
        put_small(DFC1B, jnp.sum(dpre.astype(F32), 0, keepdims=True))
        R.part1[at, :] = dot(dpre, R.w1[...], 1, 1).astype(BF16)

    loop(plan.blocks, head_back)
    sum2 = SumMp(R.part1, R.sums, 3, R.all2)
    sum2.start()
    gather_sets[1].forward()
    ends.append(sum2.first)
    dtext = scale * R.dtext[...]
    text_unit = cap * cap_factor
    R.capg[...] = cap_factor * (
        dtext - text_unit * jnp.sum(text_unit * dtext, -1, keepdims=True)
    )
    store("capg", "cap_out")

    sum2.middle()
    gather_uk.forward()
    gather_pc.forward()
    gather_sets[1].wait()
    bulk(1)
    to_far[0][1].start()
    sum2.turn()
    to_near[1].start()
    sum2.wait()

    def class_back(i):
        at = rows_at(i, plan.block)
        dmlp = R.all2[at, :].astype(F32)
        _, hat, spread = norm_rows(R.midc[at, :], row(G2), row(B2))
        dmid = R.dmid[at, :] + norm_back(dmlp, row(G2), hat, spread)
        put_small(DG2, jnp.sum(dmlp * hat, 0, keepdims=True))
        put_small(DB2, jnp.sum(dmlp, 0, keepdims=True))
        put_small(DOUTB, jnp.sum(dmid, 0, keepdims=True))
        R.dmid[at, :] = dmid
        dlow = dmid.astype(BF16)
        put("dmidl", i, dlow)
        R.dctx[at, :] = dot(dlow, R.wo[rows_at(mp, local), :], 1, 1).astype(BF16)

    loop(plan.blocks, class_back)
    store("dctx")

    dx = spread_heads(R.dctx[mine, :])
    probs = R.probs[...]
    dprobs = dot(dx, R.v[...], 1, 1)
    dscores = probs * (dprobs - jnp.sum(probs * dprobs, -1, keepdims=True))
    dscores = (dscores * 0.125).astype(BF16)
    R.arow[...] = dot(dscores, R.attn[...]).astype(BF16)
    gather_a = GatherDpTwice(R.a_out, hg, R.arow)
    gather_a.start()
    ends.append(load(R.arow, R.a_out.at[rows_at(dp, hg)]))
    dq = join_heads(dot(dscores, R.k[...])).astype(BF16)
    R.u[late, :] = dot(dx, R.wt[2 * local : 3 * local, :]).astype(BF16)
    gather_uv = GatherMp(lambda i: R.u.at[rows_at(mps + i, hg)])
    gather_uv.start()
    R.coef[rows_at(mp, hg), :] = dot(dscores, fold).astype(BF16)
    R.uq[rows_at(mp, group), :] = dot(dq, R.wt[0:local, :]).astype(BF16)
    gather_dc = GatherMp(lambda i: R.coef.at[rows_at(i, hg)])
    gather_uq = GatherMp(lambda i: R.uq.at[rows_at(i, group)])
    gather_dc.start()
    gather_uq.start()
    put_small(DQB, jnp.sum(dq.astype(F32), 0, keepdims=True))
    prob_sum = jnp.sum(R.plow[...].astype(F32), -1, keepdims=True)
    put_small(DVB, jnp.sum(dx.astype(F32) * prob_sum, 0, keepdims=True))
    gather_pc.wait()
    shape = (mps * hg, rows)
    fits = lax.rem(iota(shape, 0), group) == lax.rem(iota(shape, 1), group)

    def by_rows(first):
        coef = R.coef[first : first + mps * hg, :]
        wide = jnp.where(fits, dot(coef, fold, 1, 1), 0.0).astype(BF16)
        return dot(wide, R.hat[...])

    by_probs = by_rows(mps * hg)
    chip_sum(1)
    for move in to_far[1]:
        move.start()
    gather_uv.forward()
    gather_dc.forward()
    gather_uq.forward()
    for g in (gather_uk, gather_uv, gather_dc, gather_uq):
        g.wait()
    gather_a.forward(1)

    query = R.uq[0:group, :].astype(F32)
    for m in range(1, mps):
        query += R.uq[m * group : (m + 1) * group, :].astype(F32)
    factors = R.u[...].astype(F32)
    weight = jnp.sum(R.coef[...].astype(F32), -1, keepdims=True)
    summed = jnp.concatenate([by_rows(0), by_probs], 0)
    scaled = jnp.sum(factors * summed, 0, keepdims=True)
    scaled += jnp.sum(query * R.hat[0:group, :].astype(F32), 0, keepdims=True)
    shift = jnp.sum(factors * weight, 0, keepdims=True) + jnp.sum(query, 0, keepdims=True)
    put_small(DG1, scaled)
    put_small(DB1, shift)
    spans = []
    for i, count in ((DG1, width), (DB1, width), (DQB, local), (DVB, local)):
        spans += [(i, c, min(128, count - c)) for c in range(0, count, 128)]
    tile = []
    for i, c, size_c in spans:
        piece = R.small[i : i + 1, c : c + size_c]
        tile.append(jnp.pad(piece, ((0, 0), (0, 128 - size_c))))
    R.tot[rows_at(dp, 16), :] = jnp.concatenate(tile, 0).astype(BF16)
    gather_tot = GatherDp(R.tot, 16)
    gather_tot.start()

    def spread_coef(i):
        at = rows_at(i, 2 * size)
        pick = jnp.where(
            iota((2 * size, 128), 0) // group + i * (2 * size // group)
            == iota((2 * size, 128), 1),
            1.0,
            0.0,
        ).astype(BF16)
        wide = dot(pick, R.coef[...], 1, 1)
        shape = wide.shape
        fits = lax.rem(iota(shape, 0), group) == lax.rem(iota(shape, 1), group)
        R.mid[at, :] = dot(jnp.where(fits, wide, 0.0).astype(BF16), R.u[...])

    gather_a.forward(2)
    loop(2, spread_coef)
    R.mid[0:group, :] += query
    gather_a.forward(3)
    def first_back(i):
        at = rows_at(i, step)
        hat = R.hat[at, :].astype(F32)
        R.attn[at, :] = norm_back(R.mid[at, :], row(G1), hat, R.spread[at, :]).astype(BF16)

    for i in range(mps):
        loop(size // step, lambda t, i=i: first_back(t + i * (size // step)))
        at = pl.ds(i * size, size)
        if i == 0:
            top = R.attn[0:group, :].astype(F32) + R.dmid[mine, :]
            R.attn[0:group, :] = top.astype(BF16)
        ends.append(load(R.attn.at[at], R.images_out.at[at]))

    finish(0)
    finish(1)
    gather_tot.wait()

    R.sums_left[...] = jnp.zeros((16, 128), F32)

    def add_up(i):
        R.sums_left[...] += R.tot[rows_at(i, 16), :].astype(F32)

    loop(dps, add_up)
    for n, (i, c, size_c) in enumerate(spans):
        R.small[i : i + 1, c : c + size_c] = R.sums_left[n : n + 1, 0:size_c]
    store("small")
    ends.append(load(cg, R.ctx_out))
    gather_b.wait()
    for i in range(2):
        for n, p in enumerate(pieces[i]):
            blk_near[i][n].wait_recv()
            store_rows(others[i], p)
    gather_a.wait()
    ends.extend([*to_near, *to_far[0], *to_far[1], *blk_near[0], *blk_near[1]])
    settle(len(ends))


def run_kernel(plan, *operands):
    anywhere = pl.BlockSpec(memory_space=pl.ANY)
    return pl.pallas_call(
        functools.partial(kernel, plan),
        out_shape=[jax.ShapeDtypeStruct(s, t) for s, t in plan.results().values()],
        in_specs=[anywhere] * len(plan.operands()),
        out_specs=[anywhere] * len(plan.results()),
        scratch_shapes=[pltpu.VMEM(s, t) for s, t in plan.scratch().values()]
        + [pltpu.SemaphoreType.DMA((plan.semaphores(),))],
        compiler_params=pltpu.CompilerParams(
            collective_id=0, has_side_effects=True, vmem_limit_bytes=62 << 20
        ),
    )(*operands)


def final_operands(plan):
    names = ("images", "block", "cap", "small", "post", "demb", "act", "dy", "mlp", "dpre")
    names += ("ctx", "dmid", "a", "b", "dctx", "ac", "qa")
    return {n: plan.results()[n + "_out"] for n in names}


def final_results(plan):
    d, loc, hid = plan.width, plan.local, plan.hidden
    return dict(
        loss=((1,), F32),
        block=((plan.rows, d), BF16),
        images=((plan.rows, d), F32),
        g1=((d,), F32),
        b1=((d,), F32),
        wt=((3 * loc, d), F32),
        qvb=((2, loc), F32),
        wo=((loc, d), F32),
        ob=((d,), F32),
        g2=((d,), F32),
        b2=((d,), F32),
        w1=((d, hid), F32),
        f1b=((hid,), F32),
        w2=((hid, d), F32),
        f2b=((d,), F32),
        pg=((d,), F32),
        pb=((d,), F32),
        wp=((d, plan.emb), F32),
        cap=((plan.own, plan.emb), F32),
        ls=((1,), F32),
    )


STRAIGHT = ("block", "cap")


def final_kernel(plan, *refs):
    taken, given = final_operands(plan), final_results(plan)
    given_scratch = [n for n in given if n not in STRAIGHT]
    sems = refs[-1]
    I = Named(zip((*taken, "wt"), refs))
    refs = refs[len(taken) + 1 :]
    O = Named(zip(given, refs))
    rest = refs[len(given) :]
    L = Named(zip((*taken, "wk", "dq"), rest))
    S = Named(zip(given_scratch, rest[len(taken) + 2 :]))
    used, ends, free = iter(range(40)), [], []

    def copy(src, dst):
        place = free.pop() if free else next(used)
        move = pltpu.make_async_copy(src, dst, sems.at[place])
        move.start()

        def wait():
            move.wait()
            free.append(place)

        return wait

    late = ("images", "block", "cap", "small")
    order = ("act", "dy", "mlp", "dpre", *(n for n in taken if n not in late), *late)
    local = plan.local
    loads = {"wk": copy(I.wt.at[pl.ds(local, local)], L.wk)}
    loads |= {n: copy(I[n], L[n]) for n in dict.fromkeys(order)}

    def product(name, left, right, at=0, fix=None):
        for n in (left, right):
            if n in loads:
                loads.pop(n)()
        size = L[left].shape[1]
        step = 128 if size % 128 == 0 else size
        for c in range(0, size, step):
            a, b = L[left][:, c : c + step], L[right][...]
            rows = pl.ds(at + c, step)
            S[name][rows, :] = dot(fix(a) if fix else a, b, 0, 0)
            ends.append(copy(S[name].at[rows], O[name].at[rows]))

    group, heads = plan.group, plan.heads

    def spread_heads(t):
        pieces = []
        lane = iota((group, local), 1) // HEAD_DIM
        t = t.astype(F32)
        for i in range(plan.dps):
            for h in range(heads):
                pieces.append(jnp.where(lane == h, t[i * group : (i + 1) * group], 0.0))
        return jnp.concatenate(pieces, 0).astype(BF16)

    product("w2", "act", "dy")
    product("w1", "mlp", "dpre")
    product("wp", "post", "demb")
    loads.pop("images")()
    for i in range(plan.mps):
        rows = pl.ds(i * plan.quarter, plan.quarter)
        S.images[rows, :] = L.images[rows, :].astype(F32)
        ends.append(copy(S.images.at[rows], O.images.at[rows]))
    product("wo", "ctx", "dmid")
    loads.pop("block")()
    ends.append(copy(L.block, O.block))
    product("wt", "dctx", "b", 2 * local, spread_heads)
    product("wt", "qa", "a", local, spread_heads)
    loads.pop("wk")()
    wide = dot(L.a[...], L.wk[...], 1, 1)
    lane = iota((group, local), 1) // HEAD_DIM
    for i in range(plan.dps):
        total = jnp.zeros((group, local), F32)
        for h in range(heads):
            first = (i * heads + h) * group
            total += jnp.where(lane == h, wide[first : first + group], 0.0)
        L.dq[i * group : (i + 1) * group, :] = total.astype(BF16)
    product("wt", "dq", "ac")
    loads.pop("cap")()
    ends.append(copy(L.cap, O.cap))
    loads.pop("small")()
    small = L.small
    S.loss[...] = small[LOSS, 0:1]
    S.ls[...] = small[LOSS, 128:129]
    S.qvb[...] = small[DQB : DVB + 1, 0:local]
    vectors = dict(g1=DG1, b1=DB1, ob=DOUTB, g2=DG2, b2=DB2, f1b=DFC1B, f2b=DFC2B, pg=DPG, pb=DPB)
    for n, i in vectors.items():
        S[n][...] = small[i, 0 : S[n].shape[0]]
    for n in ("loss", "ls", "qvb", *vectors):
        ends.append(copy(S[n], O[n]))
    for end in ends:
        end()


def run_final(plan, got, wt):
    taken, given = final_operands(plan), final_results(plan)
    anywhere = pl.BlockSpec(memory_space=pl.ANY)
    scratch = [*taken.values(), ((plan.local, plan.width), BF16), ((plan.images, plan.local), BF16)]
    scratch += [st for n, st in given.items() if n not in STRAIGHT]
    out = pl.pallas_call(
        functools.partial(final_kernel, plan),
        out_shape=[jax.ShapeDtypeStruct(s, t) for s, t in given.values()],
        in_specs=[anywhere] * (len(taken) + 1),
        out_specs=[anywhere] * len(given),
        scratch_shapes=[pltpu.VMEM(s, t) for s, t in scratch]
        + [pltpu.SemaphoreType.DMA((40,))],
        compiler_params=pltpu.CompilerParams(vmem_limit_bytes=60 << 20),
    )(*(got[n + "_out"] for n in taken), wt)
    return dict(zip(given, out))


def body(
    images,
    ln1_gain,
    ln1_bias,
    w_qkv,
    qv_bias,
    w_out,
    out_bias,
    ln2_gain,
    ln2_bias,
    w_fc1,
    fc1_bias,
    w_fc2,
    fc2_bias,
    post_gain,
    post_bias,
    w_proj,
    captions,
    logit_scale,
    caption_counts,
    positives,
):
    sizes = (lax.axis_size("dp"), lax.axis_size("mp"))
    plan = Plan(sizes, images, w_qkv, w_fc1, w_proj, captions, positives)

    x = jnp.transpose(images, (1, 0, 2)).reshape(plan.rows, plan.width)
    wt = jnp.transpose(w_qkv, (1, 2, 0)).reshape(3 * plan.local, plan.width)

    got = run_kernel(
        plan,
        *(x, wt, w_out, w_fc1, w_fc2, w_proj, captions),
        jnp.transpose(positives),
        caption_counts,
        *(ln1_gain, ln1_bias, ln2_gain, ln2_bias, out_bias, fc2_bias),
        *(post_gain, post_bias, fc1_bias, qv_bias, logit_scale),
    )
    out = run_final(plan, dict(zip(plan.results(), got)), wt)

    def as_images(t):
        return jnp.transpose(t.reshape(plan.seq, plan.group, plan.width), (1, 0, 2))

    out["block"], out["images"] = as_images(out["block"]), as_images(out["images"])
    out["wt"] = jnp.transpose(out["wt"].reshape(3, plan.local, plan.width), (2, 0, 1))
    return tuple(out.values())


def solution(mesh):
    full, per_dp = P(), P("dp")
    return jax.shard_map(
        body,
        mesh=mesh,
        in_specs=(
            P("dp", None, None),
            full,
            full,
            P(None, None, "mp"),
            P(None, "mp"),
            P("mp", None),
            full,
            full,
            full,
            P(None, "mp"),
            P("mp"),
            P("mp", None),
            full,
            full,
            full,
            full,
            P("dp", None),
            full,
            per_dp,
            P("dp", None),
        ),
        out_specs=(
            full,
            P("dp", None, None),
            P("dp", None, None),
            full,
            full,
            P(None, None, "mp"),
            P(None, "mp"),
            P("mp", None),
            full,
            full,
            full,
            P(None, "mp"),
            P("mp"),
            P("mp", None),
            full,
            full,
            full,
            full,
            P("dp", None),
            full,
        ),
        check_vma=False,
    )
```

profile of v0, /device:TPU:0, one launch (start us, length us, event | category | flops | bytes accessed | tf_op | source)
XLA Modules:
  0.0 58.3 jit_solution(13347223699608216790)
XLA Ops:
  1.3 50.2 %shard_map.347 = (bf16[832,768]{1,0:T(8,128)(2,1)}, bf16[832,768]{1,0:T(8,128)(2,1)}, f32[16,768]{1,0:T(8,128)}, f32[48,512]{1,0:T(8,128)}, bf16[128,768]{1,0:T(...) custom-call(bf16[832,768]{1,0:T(8,128)(2,1)} %bitcast.18, ...), custom_call_target="tpu_custom_call" | custom-call | tf_op jit(solution)/shard_map/pallas_call | solution.py:1002
  51.5 6.6 %shard_map.348 = (f32[1]{0:T(128)}, bf16[832,768]{1,0:T(8,128)(2,1)}, f32[832,768]{1,0:T(8,128)}, f32[768]{0:T(1024)}, f32[768]{0:T(1024)}, /*index=5*/f32[576,7...) custom-call(bf16[832,768]{1,0:T(8,128)(2,1)} %get-tuple-element.57.r, ...), custom_call_target="tpu_custom_call" | custom-call | tf_op jit(solution)/shard_map/pallas_call | solution.py:1146
where the time goes:
time: 58.7 us; the launch traced here: 58.3 us
  Pallas kernels  56.8 us (97%)
  between operations  1.5 us (3%)
    pallas_call x1, Pallas kernels, run_kernel(): pl.pallas_call(functools.partial(kernel, plan), out_shape=[jax.ShapeDtype...  50.2 us
    pallas_call x1, Pallas kernels, run_final(): pl.pallas_call(functools.partial(final_kernel, plan), out_shape=[jax.Shap...  6.58 us

commit v1 on v0

--- a/solution.py
+++ b/solution.py
@@ -61,7 +61,7 @@
     __getattr__ = dict.__getitem__
 
 
-SEMS = 119
+SEMS = 110
 
 
 class Plan:
@@ -164,8 +164,7 @@
             v1=((64 * self.group, 128), F32),
             probs=((hg, r), F32),
             plow=((hg, r), BF16),
-            ca=((m, r, 128), BF16),
-            cb=((m, r // 2, 128), BF16),
+            cx=((m, 2, 3 * self.quarter, 128), BF16),
             mid=((r, d), F32),
             midq=((2, r // m, d), F32),
             part=((r, d), BF16),
@@ -580,34 +579,13 @@
     gather_cg.start()
     loop(group // 4 - first_part, lambda t: attend(t + first_part))
     quarter = plan.quarter
-    for i, index in enumerate((0, 2, 1, 3)):
-        taken_rows = R.q0[index * quarter : (index + 1) * quarter, :]
-        R.ca[mp, i * quarter : (i + 1) * quarter, :] = taken_rows.astype(BF16)
-    R.cb[mp] = jnp.concatenate(
-        [R.q1[0 : rows // 2, 0:64], R.q1[rows // 2 : rows, 0:64]], 1
-    ).astype(BF16)
-
-    class GatherSet:
-        def __init__(self, i):
-            wide, packed = pl.ds(2 * i * quarter, 2 * quarter), pl.ds(i * quarter, quarter)
-            self.parts = (
-                GatherMp(lambda m: R.ca.at[m, wide]),
-                GatherMp(lambda m: R.cb.at[m, packed]),
-            )
-
-        def start(self):
-            for part in self.parts:
-                part.start()
-
-        def forward(self):
-            for part in self.parts:
-                part.forward()
-
-        def wait(self):
-            for part in self.parts:
-                part.wait()
-
-    gather_sets = [GatherSet(i) for i in range(2)]
+    for i in range(2):
+        both = [slice((i + 2 * n) * quarter, (i + 2 * n + 1) * quarter) for n in range(2)]
+        for n, at in enumerate(both):
+            R.cx[mp, i, n * quarter : (n + 1) * quarter, :] = R.q0[at, :].astype(BF16)
+        last = jnp.concatenate([R.q1[at, 0:64] for at in both], 1)
+        R.cx[mp, i, 2 * quarter : 3 * quarter, :] = last.astype(BF16)
+    gather_sets = [GatherMp(lambda m, i=i: R.cx.at[m, i]) for i in range(2)]
     gather_uk = GatherMp(lambda i: R.u.at[rows_at(i, hg)])
     gather_pc = GatherMp(lambda i: R.coef.at[rows_at(mps + i, hg)])
     gather_xc.relay()
@@ -649,19 +627,18 @@
 
     size = plan.quarter
 
-    def joined_context(index):
-        side, which = lax.div(index, 2), lax.rem(index, 2)
-        joined = []
+    def joined_context(index, i):
+        side, joined = lax.div(index, 2), []
         for m in range(mps):
-            tail = R.cb[m, rows_at(which, size), :].astype(F32)
+            tail = R.cx[m, i, 2 * size : 3 * size, :].astype(F32)
             tail = jnp.where(side == 0, tail[:, 0:64], tail[:, 64:128])
-            joined += [R.ca[m, rows_at(2 * which + side, size), :].astype(F32), tail]
+            joined += [R.cx[m, i, rows_at(side, size), :].astype(F32), tail]
         return jnp.concatenate(joined, 1).astype(BF16)
 
     def bulk(i):
         at = [rows_at(index, size) for index in (others[i], owned[i])]
         total = jnp.concatenate([R.x[a, :].astype(F32) for a in at], 0) + row(OUTB)
-        joined = [joined_context(index) for index in (others[i], owned[i])]
+        joined = [joined_context(index, i) for index in (others[i], owned[i])]
         total += dot(jnp.concatenate(joined, 0), R.wo[...])
         R.midq[i] = total[size : 2 * size]
         mlp = norm_rows(total, row(G2), row(B2))[0].astype(BF16)
@@ -1073,8 +1050,8 @@
     late = ("images", "block", "cap", "small")
     order = ("act", "dy", "mlp", "dpre", *(n for n in taken if n not in late), *late)
     local = plan.local
-    loads = {"wk": copy(I.wt.at[pl.ds(local, local)], L.wk)}
-    loads |= {n: copy(I[n], L[n]) for n in dict.fromkeys(order)}
+    loads = {n: copy(I[n], L[n]) for n in dict.fromkeys(order)}
+    loads["wk"] = copy(I.wt.at[pl.ds(local, local)], L.wk)
 
     def product(name, left, right, at=0, fix=None):
         for n in (left, right):

time: 58.7 us -> 58.5 us (level)
  no operation moved by 1% of the time
where the time goes in v1:
time: 58.5 us; the launch traced here: 58 us
  Pallas kernels  56.5 us (97%)
  between operations  1.5 us (3%)
    pallas_call x1, Pallas kernels, run_kernel(): pl.pallas_call(functools.partial(kernel, plan), out_shape=[jax.ShapeDtype...  49.9 us
    pallas_call x1, Pallas kernels, run_final(): pl.pallas_call(functools.partial(final_kernel, plan), out_shape=[jax.Shap...  6.61 us

profile of v1, /device:TPU:0, one launch (start us, length us, event | category | flops | bytes accessed | tf_op | source)
XLA Modules:
  0.0 58.0 jit_solution(11045388552121232145)
XLA Ops:
  1.3 49.9 %shard_map.347 = (bf16[832,768]{1,0:T(8,128)(2,1)}, bf16[832,768]{1,0:T(8,128)(2,1)}, f32[16,768]{1,0:T(8,128)}, f32[48,512]{1,0:T(8,128)}, bf16[128,768]{1,0:T(...) custom-call(bf16[832,768]{1,0:T(8,128)(2,1)} %bitcast.18, ...), custom_call_target="tpu_custom_call" | custom-call | tf_op jit(solution)/shard_map/pallas_call | solution.py:979
  51.2 6.6 %shard_map.348 = (f32[1]{0:T(128)}, bf16[832,768]{1,0:T(8,128)(2,1)}, f32[832,768]{1,0:T(8,128)}, f32[768]{0:T(1024)}, f32[768]{0:T(1024)}, /*index=5*/f32[576,7...) custom-call(bf16[832,768]{1,0:T(8,128)(2,1)} %get-tuple-element.57.r, ...), custom_call_target="tpu_custom_call" | custom-call | tf_op jit(solution)/shard_map/pallas_call | solution.py:1123

commit v2 on v1

--- a/solution.py
+++ b/solution.py
@@ -1085,10 +1085,10 @@
         S.images[rows, :] = L.images[rows, :].astype(F32)
         ends.append(copy(S.images.at[rows], O.images.at[rows]))
     product("wo", "ctx", "dmid")
+    product("wt", "dctx", "b", 2 * local, spread_heads)
+    product("wt", "qa", "a", local, spread_heads)
     loads.pop("block")()
     ends.append(copy(L.block, O.block))
-    product("wt", "dctx", "b", 2 * local, spread_heads)
-    product("wt", "qa", "a", local, spread_heads)
     loads.pop("wk")()
     wide = dot(L.a[...], L.wk[...], 1, 1)
     lane = iota((group, local), 1) // HEAD_DIM

time: 58.5 us -> 58.2 us (level)
  no operation moved by 1% of the time
where the time goes in v2:
time: 58.2 us; the launch traced here: 57.7 us
  Pallas kernels  56.2 us (97%)
  between operations  1.5 us (3%)
    pallas_call x1, Pallas kernels, run_kernel(): pl.pallas_call(functools.partial(kernel, plan), out_shape=[jax.ShapeDtype...  49.9 us
    pallas_call x1, Pallas kernels, run_final(): pl.pallas_call(functools.partial(final_kernel, plan), out_shape=[jax.Shap...  6.3 us

profile of v2, /device:TPU:0, one launch (start us, length us, event | category | flops | bytes accessed | tf_op | source)
XLA Modules:
  0.0 57.7 jit_solution(665327399318885006)
XLA Ops:
  1.3 49.9 %shard_map.347 = (bf16[832,768]{1,0:T(8,128)(2,1)}, bf16[832,768]{1,0:T(8,128)(2,1)}, f32[16,768]{1,0:T(8,128)}, f32[48,512]{1,0:T(8,128)}, bf16[128,768]{1,0:T(...) custom-call(bf16[832,768]{1,0:T(8,128)(2,1)} %bitcast.18, ...), custom_call_target="tpu_custom_call" | custom-call | tf_op jit(solution)/shard_map/pallas_call | solution.py:979
  51.2 6.3 %shard_map.348 = (f32[1]{0:T(128)}, bf16[832,768]{1,0:T(8,128)(2,1)}, f32[832,768]{1,0:T(8,128)}, f32[768]{0:T(1024)}, f32[768]{0:T(1024)}, /*index=5*/f32[576,7...) custom-call(bf16[832,768]{1,0:T(8,128)(2,1)} %get-tuple-element.57.r, ...), custom_call_target="tpu_custom_call" | custom-call | tf_op jit(solution)/shard_map/pallas_call | solution.py:1123
